TPU v7x, 32 devices: a whole 2x2x4 slice. The times are simulated.
32 devices in a mesh: rep: 2 (over x), grp: 4 (over z), tp: 4 (over y, core).
Axes of the slice: x: 2, y: 2, z: 4, core: 2. Of those that a mesh axis runs over, the one named last changes fastest.
Arguments:
- x_in: bfloat16 [4, 8, 128, 1280], P(None, ('rep', 'grp'), None, 'tp'), parts along dimension 1, may hold values from -6 to 6
- taps: bfloat16 [4, 8, 128, 6400], P(None, ('rep', 'grp'), None, 'tp'), parts along dimension 1, may hold values from -6 to 6
- ln_gain: float32 [1280], replicated, may hold values from 0.1 to 1.9
- ln_bias: float32 [1280], replicated, may hold values from -3 to 3
- w_up: bfloat16 [1280, 5120], P(None, 'tp'), may hold values from -0.15625 to 0.15625
- b_up: float32 [5120], P('tp'), may hold values from -3 to 3
- w_down: bfloat16 [5120, 1280], P('tp'), may hold values from -0.078125 to 0.078125
- b_down: float32 [1280], P('tp'), may hold values from -3 to 3
- kv_w_out: bfloat16 [1280, 2048], P('tp'), may hold values from -0.0625 to 0.0625
- kv_w_taps: bfloat16 [6400, 2048], P('tp'), may hold values from -0.09375 to 0.09375
- k_gain: float32 [128], replicated, may hold values from 1 to 2.5
- q_gain: float32 [128], replicated, may hold values from 1 to 2.5
- queries: bfloat16 [4096, 8192], P(('rep', 'grp'), 'tp'), parts along dimension 0, may hold values from -6 to 6
- tiles_per_request: int32 [16], P('rep'), parts along dimension 0, may hold values from 1 to 4, as said below
- owner: int32 [16], P('rep'), parts along dimension 0, may hold values from 0 to 3, as said below
- text_per_request: int32 [16], P('rep'), parts along dimension 0, may hold values from 64 to 256, as said below
Outputs:
- attended: bfloat16 [4096, 8192], P(('rep', 'grp'), 'tp'), parts along dimension 0
There are 2 independent parts, one for each index of `rep`. A program takes and returns all parts, laid end to end along the dimension named above; an argument that names none is the same for every part. Nothing has to cross between parts.
Inputs may be any that keep to these rules, and one draw needn't show every extreme that they name: `owner`: each group owns exactly 2 requests. `tiles_per_request`: the tiles of all requests sum to 16; the tiles of one group's requests sum to at most 8, and some group has exactly 8. `text_per_request`: the text tokens of one group's requests sum to at most 512, and some group has exactly 512.
All inputs are finite; a program needn't handle non-finite values.
Results may differ from a plain program's by a relative error of at most 0.04.
Values may be sent and summed in bfloat16 or wider, within the bound.
A program may use at most 128 MiB of HBM per device.

v0:
```python
import functools

import jax
import jax.numpy as jnp
from jax import lax
from jax.experimental import pallas as pl
from jax.experimental.pallas import tpu as pltpu
from jax.sharding import PartitionSpec as P

KVH = 8
HD = 128
MAXT = 4
REQ_G = 2
CAP = REQ_G * MAXT

epsilon = 1e-05
MESH = pl.DeviceIdType.MESH
VMEM_BYTES = 60 * 1024 * 1024
LOG2E = 1.4426950408889634
V_SCALE = 2.0**-14
F32 = jnp.float32
BF16 = jnp.bfloat16


def fused_kernel(
    sizes,
    x_hbm,
    taps_hbm,
    gain_ref,
    bias_ref,
    wup_hbm,
    bup_ref,
    wdn_hbm,
    bdn_ref,
    wko_hbm,
    wkt_hbm,
    kgain_ref,
    qgain_ref,
    q_hbm,
    tiles_ref,
    owner_ref,
    text_ref,
    out_hbm,
    xg,
    normed,
    hidden,
    tapst,
    taps,
    wup,
    wdn,
    wko,
    wkt,
    kvt,
    encoded,
    m_send,
    m_r1,
    m_s2,
    m_r2,
    k_send,
    k_r1,
    k_s2,
    k_r2,
    kwin,
    vwin,
    qbuf,
    obuf,
    *rest,
):
    tp_n, grp_n, nch, chan, kv_heads = sizes
    kvs, sems = rest[:kv_heads], rest[kv_heads:]
    (
        w_sem,
        x_ssem,
        x_rsem,
        xp_ssem,
        xp_rsem,
        l1_ssem,
        l1_rsem,
        l2_ssem,
        l2_rsem,
        z_ssem,
        z_rsem,
        o_sem,
    ) = sems
    places, depth, tile = xg.shape
    total_tiles = places * grp_n
    per = places // nch
    rc = per * tile
    chips = tp_n // 2
    order = sorted(range(places), key=lambda k: (abs(2 * k - (places - 1)), k))
    tp_i = lax.axis_index("tp")
    grp_i = lax.axis_index("grp")
    core = lax.rem(tp_i, 2)
    chip = tp_i // 2
    other = 1 - core
    partner = {"tp": chip * 2 + other}

    def peer(dy):
        return lax.rem(chip + dy, chips)

    def peer_id(dy):
        return {"tp": peer(dy) * 2 + core}

    def share(slot):
        return pl.ds(pl.multiple_of(slot * chan, 16), chan)

    names = ["taps", "wkt", "wup", "wdn", "q", "wko"]
    sources = [
        (taps_hbm, tapst),
        (wkt_hbm, wkt),
        (wup_hbm, wup),
        (wdn_hbm, wdn),
        (q_hbm, qbuf),
        (wko_hbm, wko),
    ]
    loads = {
        name: pltpu.make_async_copy(src, dst, w_sem.at[i])
        for i, (name, (src, dst)) in enumerate(zip(names, sources))
    }
    own_x = [
        pltpu.make_async_copy(x_hbm.at[order[pos]], xg.at[pos, share(tp_i)], w_sem.at[6 + pos])
        for pos in range(places)
    ]
    for c in own_x:
        c.start()
    for name in names:
        loads[name].start()

    barrier = pltpu.get_barrier_semaphore()
    pl.semaphore_signal(barrier, inc=1, device_id=partner, device_id_type=MESH)
    for dy in range(1, chips):
        pl.semaphore_signal(barrier, inc=1, device_id=peer_id(dy), device_id_type=MESH)

    @pl.when(grp_i > 0)
    def _():
        pl.semaphore_signal(barrier, inc=1, device_id={"grp": grp_i - 1}, device_id_type=MESH)

    @pl.when(grp_i < grp_n - 1)
    def _():
        pl.semaphore_signal(barrier, inc=1, device_id={"grp": grp_i + 1}, device_id_type=MESH)

    neighbours = jnp.where(grp_i > 0, 1, 0) + jnp.where(grp_i < grp_n - 1, 1, 0)
    pl.semaphore_wait(barrier, chips + neighbours)

    def rows(ch):
        return pl.ds(ch * rc, rc)

    def x_copy(pos, dy):
        return pltpu.make_async_remote_copy(
            src_ref=x_hbm.at[order[pos]],
            dst_ref=xg.at[pos, share(tp_i)],
            send_sem=x_ssem.at[pos, dy],
            recv_sem=x_rsem.at[pos, dy],
            device_id=peer_id(dy) if dy else partner,
            device_id_type=MESH,
        )

    def x_pass(pos, dy):
        slot = lax.rem(chip - dy + chips, chips) * 2 + core
        return pltpu.make_async_remote_copy(
            src_ref=xg.at[pos, share(slot)],
            dst_ref=xg.at[pos, share(slot)],
            send_sem=xp_ssem.at[pos, dy],
            recv_sem=xp_rsem.at[pos, dy],
            device_id=partner,
            device_id_type=MESH,
        )

    def x_forward(pos):
        for dy in range(1, chips):
            x_copy(pos, dy).wait_recv()
            x_pass(pos, dy).start()

    for pos in range(places):
        for dy in list(range(1, chips)) + [0]:
            x_copy(pos, dy).start()

    def head_start(t, h):
        return (t * KVH // tp_n + h) * (2 * HD)

    kv_cols = kvt.shape[1]
    step = 2 * HD

    def tap_rows(pos):
        taps[pos * tile : (pos + 1) * tile, :] = tapst[order[pos]].T

    def tap_product(piece, pieces):
        count = kv_cols // step // pieces

        def body(j, carry):
            at = piece * count + j
            block = lax.rem(at * kv_heads, kv_cols // step) + at * kv_heads // (kv_cols // step)
            cols = pl.ds(pl.multiple_of(block * step, step), step)
            kvt[:, cols] = jnp.dot(taps[...], wkt[:, cols], preferred_element_type=F32)
            return carry

        lax.fori_loop(0, count, body, 0)

    units = hidden.shape[1]

    def up(ch):
        for pos in range(ch * per, (ch + 1) * per):
            own_x[pos].wait()
            x_copy(pos, 0).wait_recv()
            for dy in range(1, chips):
                x_pass(pos, dy).wait_recv()
            blocks = [slice(b * HD, (b + 1) * HD) for b in range(depth // HD)]
            total = jnp.zeros((8, tile), F32)
            for b in blocks:
                values = xg[pos, b, :].astype(F32)
                total = total + jnp.sum(values.reshape(HD // 8, 8, tile), axis=0)
            average = jnp.sum(total, axis=0, keepdims=True) / depth
            square = jnp.zeros((8, tile), F32)
            for b in blocks:
                centered = xg[pos, b, :].astype(F32) - average
                square = square + jnp.sum((centered * centered).reshape(HD // 8, 8, tile), axis=0)
            factor = lax.rsqrt(jnp.sum(square, axis=0, keepdims=True) / depth + epsilon)
            inside = slice((pos - ch * per) * tile, (pos - ch * per + 1) * tile)
            for b in blocks:
                scaled = ((xg[pos, b, :].astype(F32) - average) * factor).T
                normed[inside, b] = (
                    scaled * gain_ref[b].reshape(1, HD) + bias_ref[b].reshape(1, HD)
                ).astype(BF16)
        if ch == 0:
            loads["wup"].wait()
        for j in range(0, units, 256):
            cols = slice(j, min(j + 256, units))
            pre = jnp.dot(normed[...], wup[:, cols], preferred_element_type=F32)
            pre = pre + bup_ref[cols].reshape(1, -1)
            hidden[:, cols] = (0.5 * pre * (1.0 + lax.erf(pre * (0.5**0.5)))).astype(BF16)

    def down(ch):
        if ch == 0:
            loads["wdn"].wait()
        terms = jnp.dot(hidden[...], wdn[...], preferred_element_type=F32).astype(BF16).T
        for t in range(tp_n):
            m_send[ch, t % 2, t // 2] = terms[t * chan : (t + 1) * chan, :]

    def buffers(stage):
        which, at = stage
        if which == 0:
            return (b.at[at] for b in (m_send, m_r1, m_s2, m_r2))
        return (b.at[at] for b in (k_send, k_r1, k_s2, k_r2))

    def number(stage):
        which, at = stage
        return at if which == 0 else nch + at

    def l1(stage):
        send, r1, _, _ = buffers(stage)
        return pltpu.make_async_remote_copy(
            src_ref=send.at[other],
            dst_ref=r1,
            send_sem=l1_ssem.at[number(stage)],
            recv_sem=l1_rsem.at[number(stage)],
            device_id=partner,
            device_id_type=MESH,
        )

    def l2(stage, dy):
        _, _, s2, r2 = buffers(stage)
        return pltpu.make_async_remote_copy(
            src_ref=s2.at[dy - 1],
            dst_ref=r2.at[dy - 1],
            send_sem=l2_ssem.at[number(stage), dy - 1],
            recv_sem=l2_rsem.at[number(stage), dy - 1],
            device_id=peer_id(dy),
            device_id_type=MESH,
        )

    def level2(stage):
        send, r1, s2, _ = buffers(stage)
        l1(stage).wait_recv()
        for dy in range(1, chips):
            y = peer(dy)
            s2[dy - 1] = (send[core, y].astype(F32) + r1[y].astype(F32)).astype(BF16)
            l2(stage, dy).start()

    def summed(stage):
        send, r1, _, r2 = buffers(stage)
        total = send[core, chip].astype(F32) + r1[chip].astype(F32)
        for dy in range(1, chips):
            l2(stage, dy).wait_recv()
            total = total + r2[dy - 1].astype(F32)
        return total

    def encode(ch):
        total = summed((0, ch))
        for p in range(per):
            pos = ch * per + p
            here = total[:, p * tile : (p + 1) * tile] + xg[pos, share(tp_i), :].astype(F32)
            encoded[pos * tile : (pos + 1) * tile, :] = (
                here.T + bdn_ref[...].reshape(1, chan)
            ).astype(BF16)

    def project(h, ch):
        if h == 0 and ch == 0:
            loads["wko"].wait()
        for t in range(tp_n):
            cols = slice(head_start(t, h), head_start(t, h) + step)
            k_send[h * nch + ch, t % 2, t // 2] = (
                jnp.dot(encoded[rows(ch), :], wko[:, cols], preferred_element_type=F32)
                + kvt[rows(ch), cols]
            ).astype(BF16)
        l1((1, h * nch + ch)).start()

    def finish(h, ch):
        total = summed((1, h * nch + ch))
        key = total[:, :HD]
        square = jnp.mean(key * key, axis=-1, keepdims=True)
        key = (key * lax.rsqrt(square + epsilon) * kgain_ref[...].reshape(1, HD)).astype(BF16)
        value = total[:, HD:].astype(BF16)
        for p in range(per):
            pos = ch * per + p
            at = order[pos] * grp_n + grp_i
            kvs[h][at, :, :HD] = key[p * tile : (p + 1) * tile]
            kvs[h][at, :, HD:] = value[p * tile : (p + 1) * tile]
            z_start(h, pos, 0)

    def reaches_up(index, q):
        return (index >= REQ_G * q) & (index >= total_tiles - CAP * (grp_n - q))

    def reaches_down(index, q):
        return (index < total_tiles - REQ_G * (grp_n - 1 - q)) & (index < CAP * (q + 1))

    def z_copy(h, pos, way, k):
        block = jnp.clip(grp_i - k if way == 0 else grp_i + k, 0, grp_n - 1)
        at = order[pos] * grp_n + block
        return pltpu.make_async_remote_copy(
            src_ref=kvs[h].at[at],
            dst_ref=kvs[h].at[at],
            send_sem=z_ssem.at[h, way, pos, k],
            recv_sem=z_rsem.at[h, way, pos, k],
            device_id={"grp": grp_i + 1 if way == 0 else grp_i - 1},
            device_id_type=MESH,
        )

    def z_sends(pos, way, k):
        base = order[pos] * grp_n
        if way == 0:
            return (grp_i - k >= 0) & (grp_i < grp_n - 1) & reaches_up(base + grp_i - k, grp_i + 1)
        return (grp_i + k <= grp_n - 1) & (grp_i > 0) & reaches_down(base + grp_i + k, grp_i - 1)

    def z_gets(pos, way, k):
        base = order[pos] * grp_n
        if way == 0:
            return (grp_i - k - 1 >= 0) & reaches_up(base + grp_i - k - 1, grp_i)
        return (grp_i + k + 1 <= grp_n - 1) & reaches_down(base + grp_i + k + 1, grp_i)

    def z_start(h, pos, k):
        for way in range(2):

            @pl.when(z_sends(pos, way, k))
            def _(way=way):
                z_copy(h, pos, way, k).start()

    def z_hop(h, pos, k):
        for way in range(2):

            @pl.when(z_gets(pos, way, k))
            def _(way=way):
                z_copy(h, pos, way, k).wait_recv()

        if k + 1 < grp_n - 1:
            z_start(h, pos, k + 1)

    text_rows = qbuf.shape[0]
    q_heads = qbuf.shape[1] // HD
    per_kv = q_heads // kv_heads
    half = text_rows // REQ_G
    window = min(MAXT, total_tiles)

    offset = jnp.int32(0)
    tiles = [jnp.int32(0), jnp.int32(0)]
    texts = [jnp.int32(0), jnp.int32(0)]
    seen = jnp.int32(0)
    for r in range(owner_ref.shape[0]):
        own = owner_ref[r] == grp_i
        offset = offset + jnp.where(owner_ref[r] < grp_i, tiles_ref[r], 0)
        for i in range(REQ_G):
            here = own & (seen == i)
            tiles[i] = jnp.where(here, tiles_ref[r], tiles[i])
            texts[i] = jnp.where(here, text_ref[r], texts[i])
        seen = seen + own.astype(jnp.int32)

    def head_cols(qh):
        return pl.ds(pl.multiple_of(qh * HD, HD), HD)

    def norm_queries(low, high):
        def body(qh, carry):
            query = qbuf[:, head_cols(qh)].astype(F32)
            square = jnp.mean(query * query, axis=-1, keepdims=True)
            gain = qgain_ref[...].reshape(1, HD) * (LOG2E / float(HD) ** 0.5)
            qbuf[:, head_cols(qh)] = (query * lax.rsqrt(square + epsilon) * gain).astype(BF16)
            return carry

        lax.fori_loop(low, high, body, 0)

    def windows(h):
        for i in range(REQ_G):
            low = offset if i == 0 else offset + tiles[0]
            start = jnp.minimum(low, total_tiles - window)
            here = kvs[h][pl.ds(start, window)].reshape(window * tile, 2 * HD)
            row = lax.broadcasted_iota(jnp.int32, (window * tile, HD), 0) + start * tile
            valid = (row >= low * tile) & (row < (low + tiles[i]) * tile)
            kwin[i] = jnp.where(valid, here[:, :HD].astype(F32), 0.0).astype(BF16)
            vwin[i, :, :HD] = jnp.where(valid, here[:, HD:].astype(F32) * V_SCALE, 0.0).astype(BF16)
            vwin[i, :, HD:] = jnp.where(valid, V_SCALE, 0.0).astype(BF16)

    def scores(query, i):
        return lax.dot_general(
            query, kwin[i], (((1,), (1,)), ((), ())), preferred_element_type=F32
        )

    def attend(low, high):
        row = lax.broadcasted_iota(jnp.int32, (half, 1), 0)
        first = row < texts[0]
        live = row + half < texts[0] + texts[1]

        def body(qh, carry):
            query = qbuf[:half, head_cols(qh)]
            both = jnp.where(first, scores(query, 0), scores(query, 1))
            weights = jnp.exp2(both).astype(BF16)
            result = jnp.where(
                first,
                jnp.dot(weights, vwin[0], preferred_element_type=F32),
                jnp.dot(weights, vwin[1], preferred_element_type=F32),
            )
            top = row < texts[0] + texts[1]
            obuf[:half, head_cols(qh)] = jnp.where(top, result[:, :HD] / result[:, HD:], 0.0).astype(
                BF16
            )
            query = qbuf[half:, head_cols(qh)]
            weights = jnp.exp2(scores(query, 1)).astype(BF16)
            result = jnp.dot(weights, vwin[1], preferred_element_type=F32)
            obuf[half:, head_cols(qh)] = jnp.where(
                live, result[:, :HD] / result[:, HD:], 0.0
            ).astype(BF16)
            return carry

        lax.fori_loop(low, high, body, 0)

    def out_copy(h):
        cols = pl.ds(h * per_kv * HD, per_kv * HD)
        return pltpu.make_async_copy(obuf.at[:, cols], out_hbm.at[:, cols], o_sem.at[h])

    loads["taps"].wait()
    for pos in range(places):
        tap_rows(pos)
    loads["wkt"].wait()
    pieces = 4
    done = 0
    for pos in range(places):
        if pos % 2 == 0:
            tap_product(done, pieces)
            done += 1
        x_forward(pos)

    up(0)
    down(0)
    l1((0, 0)).start()
    for ch in range(1, nch):
        up(ch)
        level2((0, ch - 1))
        down(ch)
        l1((0, ch)).start()
    if done < pieces:
        tap_product(done, pieces)
        done += 1
    level2((0, nch - 1))
    while done < pieces:
        tap_product(done, pieces)
        done += 1
    loads["q"].wait()
    norm_queries(0, q_heads)

    stages = [(h, ch) for h in range(kv_heads) for ch in range(nch)]
    for j, (h, ch) in enumerate(stages):
        if h == 0:
            encode(ch)
        project(h, ch)
        if j > 0:
            level2((1, j - 1))
    level2((1, len(stages) - 1))

    last = grp_n - 2

    def chunk(ch):
        return range(ch * per, (ch + 1) * per)

    for h in range(kv_heads):
        if h == 0:
            for ch in range(nch):
                finish(0, ch)
            for k in range(last):
                for pos in range(places):
                    z_hop(0, pos, k)
                for ch in range(nch):
                    if kv_heads > 1 and k == ch:
                        finish(1, ch)
        if h == 0 and kv_heads > 1:
            for ch in range(last, nch):
                finish(1, ch)
        for pos in range(places):
            z_hop(h, pos, last)
        windows(h)
        base = h * per_kv
        if h + 1 < kv_heads:
            parts = last + 1
            edges = [per_kv * p // parts for p in range(parts + 1)]
            for k in range(parts):
                attend(base + edges[k], base + edges[k + 1])
                if k < last:
                    for pos in range(places):
                        z_hop(h + 1, pos, k)
        else:
            attend(base, base + per_kv)
        out_copy(h).start()

    for pos in range(places):
        for dy in range(chips):
            x_copy(pos, dy).wait_send()
        for dy in range(1, chips):
            x_pass(pos, dy).wait_send()
    for stage in [(0, ch) for ch in range(nch)] + [(1, j) for j in range(len(stages))]:
        l1(stage).wait_send()
        for dy in range(1, chips):
            l2(stage, dy).wait_send()
    for h in range(kv_heads):
        for pos in range(places):
            for k in range(grp_n - 1):
                for way in range(2):

                    @pl.when(z_sends(pos, way, k))
                    def _(h=h, pos=pos, way=way, k=k):
                        z_copy(h, pos, way, k).wait_send()

    for h in range(kv_heads):
        out_copy(h).wait()


def local(
    x_in,
    taps,
    ln_gain,
    ln_bias,
    w_up,
    b_up,
    w_down,
    b_down,
    kv_w_out,
    kv_w_taps,
    k_gain,
    q_gain,
    queries,
    tiles_per_request,
    owner,
    text_per_request,
):
    grp_n = lax.axis_size("grp")
    tp_n = lax.axis_size("tp")
    chips = tp_n // 2
    places, _, tile, chan = x_in.shape
    n = places * tile
    nch = 2 if places % 2 == 0 else 1
    rc = n // nch
    depth, units = w_up.shape
    tap_share, kv_cols = kv_w_taps.shape
    kv_heads = max(1, KVH // tp_n)
    width = 2 * HD
    stages = kv_heads * nch
    text_rows, query_width = queries.shape
    window = min(MAXT, places * grp_n) * tile
    any_spec = pl.BlockSpec(memory_space=pl.ANY)
    vmem_spec = pl.BlockSpec(memory_space=pltpu.VMEM)
    smem_spec = pl.BlockSpec(memory_space=pltpu.SMEM)
    dma = pltpu.SemaphoreType.DMA
    return pl.pallas_call(
        functools.partial(fused_kernel, (tp_n, grp_n, nch, chan, kv_heads)),
        name="fused",
        out_shape=jax.ShapeDtypeStruct(queries.shape, BF16),
        in_specs=[
            any_spec,
            any_spec,
            vmem_spec,
            vmem_spec,
            any_spec,
            vmem_spec,
            any_spec,
            vmem_spec,
            any_spec,
            any_spec,
            vmem_spec,
            vmem_spec,
            any_spec,
            smem_spec,
            smem_spec,
            smem_spec,
        ],
        out_specs=any_spec,
        scratch_shapes=[
            pltpu.VMEM((places, depth, tile), BF16),
            pltpu.VMEM((rc, depth), BF16),
            pltpu.VMEM((rc, units), BF16),
            pltpu.VMEM((places, tap_share, tile), BF16),
            pltpu.VMEM((n, tap_share), BF16),
            pltpu.VMEM(w_up.shape, BF16),
            pltpu.VMEM(w_down.shape, BF16),
            pltpu.VMEM(kv_w_out.shape, BF16),
            pltpu.VMEM(kv_w_taps.shape, BF16),
            pltpu.VMEM((n, kv_cols), F32),
            pltpu.VMEM((n, chan), BF16),
            pltpu.VMEM((nch, 2, chips, chan, rc), BF16),
            pltpu.VMEM((nch, chips, chan, rc), BF16),
            pltpu.VMEM((nch, chips - 1, chan, rc), BF16),
            pltpu.VMEM((nch, chips - 1, chan, rc), BF16),
            pltpu.VMEM((stages, 2, chips, rc, width), BF16),
            pltpu.VMEM((stages, chips, rc, width), BF16),
            pltpu.VMEM((stages, chips - 1, rc, width), BF16),
            pltpu.VMEM((stages, chips - 1, rc, width), BF16),
            pltpu.VMEM((REQ_G, window, HD), BF16),
            pltpu.VMEM((REQ_G, window, 2 * HD), BF16),
            pltpu.VMEM((text_rows, query_width), BF16),
            pltpu.VMEM((text_rows, query_width), BF16),
        ]
        + [pltpu.VMEM((places * grp_n, tile, width), BF16) for _ in range(kv_heads)]
        + [
            dma((6 + places,)),
            dma((places, chips)),
            dma((places, chips)),
            dma((places, chips)),
            dma((places, chips)),
            dma((nch + stages,)),
            dma((nch + stages,)),
            dma((nch + stages, chips - 1)),
            dma((nch + stages, chips - 1)),
            dma((kv_heads, 2, places, grp_n - 1)),
            dma((kv_heads, 2, places, grp_n - 1)),
            dma((kv_heads,)),
        ],
        compiler_params=pltpu.CompilerParams(
            collective_id=0, has_side_effects=True, vmem_limit_bytes=VMEM_BYTES
        ),
    )(
        jnp.transpose(x_in, (0, 1, 3, 2)).reshape(places, chan, tile),
        jnp.transpose(taps, (0, 1, 3, 2)).reshape(places, tap_share, tile),
        ln_gain,
        ln_bias,
        w_up,
        b_up,
        w_down,
        b_down,
        kv_w_out,
        kv_w_taps,
        k_gain,
        q_gain,
        queries,
        tiles_per_request,
        owner,
        text_per_request,
    )


def solution(mesh):
    in_specs = (
        P(None, ("rep", "grp"), None, "tp"),
        P(None, ("rep", "grp"), None, "tp"),
        P(),
        P(),
        P(None, "tp"),
        P("tp"),
        P("tp", None),
        P("tp"),
        P("tp", None),
        P("tp", None),
        P(),
        P(),
        P(("rep", "grp"), "tp"),
        P("rep"),
        P("rep"),
        P("rep"),
    )
    out_specs = P(("rep", "grp"), "tp")
    return jax.shard_map(local, mesh=mesh, in_specs=in_specs, out_specs=out_specs, check_vma=False)
```

profile of v0, /device:TPU:0, one launch (start us, length us, event | category | flops | bytes accessed | tf_op | source)
XLA Modules:
  0.0 67.4 jit_solution(11070459800508331334)
XLA Ops:
  0.0 64.2 %fused.1 = bf16[512,2048]{1,0:T(8,128)(2,1)} custom-call(bf16[4,320,128]{2,1,0:T(8,128)(2,1)} %bitcast.11, bf16[4,1600,128]{2,1,0:T(8,128)(2,1)} %bitcast.10, f32[1280]{0:T(1024)} %gain_ref.1, f32[1280]{0:T(1024)} %bias_ref.1, bf16[1280,1280]{1,0:T(8,128)(2,1)} %wup_hbm.1, f32[1280]{0:T(1024)} %bup_ref.1, bf16[1280,1280]{1,0:T(8,128)(2,1)} %wdn_hbm.1, ...), custom_call_target="tpu_custom_call" | custom-call | tf_op jit(solution)/shard_map/fused/pallas_call | solution.py:578
  64.2 3.2 %copy.20 = bf16[512,2048]{1,0:T(8,128)(2,1)} copy(bf16[512,2048]{1,0:T(8,128)(2,1)} %fused.1) | data formatting | bytes 4194304
where the time goes:
time: 67.6 us; the launch traced here: 67.4 us
  Pallas kernels  64.2 us (95%)
  local copies, waits for them, and re-layouts  3.16 us (5%)
    pallas_call x1, Pallas kernels, local(): pl.pallas_call(functools.partial(fused_kernel, (tp_n, grp_n, nch, chan, k...  64.2 us
    unnamed x1, local copies, waits for them, and re-layouts  3.16 us

commit v1 on v0

--- a/solution.py
+++ b/solution.py
@@ -40,7 +40,7 @@
     tiles_ref,
     owner_ref,
     text_ref,
-    out_hbm,
+    out_ref,
     xg,
     normed,
     hidden,
@@ -63,7 +63,9 @@
     kwin,
     vwin,
     qbuf,
-    obuf,
+    qnorm,
+    qrows,
+    orows,
     *rest,
 ):
     tp_n, grp_n, nch, chan, kv_heads = sizes
@@ -80,7 +82,6 @@
         l2_rsem,
         z_ssem,
         z_rsem,
-        o_sem,
     ) = sems
     places, depth, tile = xg.shape
     total_tiles = places * grp_n
@@ -175,30 +176,26 @@
         for dy in list(range(1, chips)) + [0]:
             x_copy(pos, dy).start()
 
-    def head_start(t, h):
-        return (t * KVH // tp_n + h) * (2 * HD)
-
     kv_cols = kvt.shape[1]
     step = 2 * HD
 
     def tap_rows(pos):
         taps[pos * tile : (pos + 1) * tile, :] = tapst[order[pos]].T
 
-    def tap_product(piece, pieces):
-        count = kv_cols // step // pieces
-
-        def body(j, carry):
-            at = piece * count + j
-            block = lax.rem(at * kv_heads, kv_cols // step) + at * kv_heads // (kv_cols // step)
+    tap_blocks = kv_cols // step
+
+    def tap_product(low, high):
+        def body(at, carry):
+            block = lax.rem(at * kv_heads, tap_blocks) + at * kv_heads // tap_blocks
             cols = pl.ds(pl.multiple_of(block * step, step), step)
             kvt[:, cols] = jnp.dot(taps[...], wkt[:, cols], preferred_element_type=F32)
             return carry
 
-        lax.fori_loop(0, count, body, 0)
+        lax.fori_loop(low, high, body, 0)
 
     units = hidden.shape[1]
 
-    def up(ch):
+    def layer_norm(ch):
         for pos in range(ch * per, (ch + 1) * per):
             own_x[pos].wait()
             x_copy(pos, 0).wait_recv()
@@ -221,10 +218,12 @@
                 normed[inside, b] = (
                     scaled * gain_ref[b].reshape(1, HD) + bias_ref[b].reshape(1, HD)
                 ).astype(BF16)
-        if ch == 0:
+
+    def up(ch, low, high):
+        if ch == 0 and low == 0:
             loads["wup"].wait()
-        for j in range(0, units, 256):
-            cols = slice(j, min(j + 256, units))
+        for j in range(low, high, 256):
+            cols = slice(j, min(j + 256, high))
             pre = jnp.dot(normed[...], wup[:, cols], preferred_element_type=F32)
             pre = pre + bup_ref[cols].reshape(1, -1)
             hidden[:, cols] = (0.5 * pre * (1.0 + lax.erf(pre * (0.5**0.5)))).astype(BF16)
@@ -235,6 +234,7 @@
         terms = jnp.dot(hidden[...], wdn[...], preferred_element_type=F32).astype(BF16).T
         for t in range(tp_n):
             m_send[ch, t % 2, t // 2] = terms[t * chan : (t + 1) * chan, :]
+        start_l1((0, ch))
 
     def buffers(stage):
         which, at = stage
@@ -246,16 +246,21 @@
         which, at = stage
         return at if which == 0 else nch + at
 
-    def l1(stage):
+    def l1(stage, dy):
         send, r1, _, _ = buffers(stage)
+        y = peer(dy)
         return pltpu.make_async_remote_copy(
-            src_ref=send.at[other],
-            dst_ref=r1,
-            send_sem=l1_ssem.at[number(stage)],
-            recv_sem=l1_rsem.at[number(stage)],
+            src_ref=send.at[other, y],
+            dst_ref=r1.at[y],
+            send_sem=l1_ssem.at[number(stage), dy],
+            recv_sem=l1_rsem.at[number(stage), dy],
             device_id=partner,
             device_id_type=MESH,
         )
+
+    def start_l1(stage):
+        for dy in list(range(1, chips)) + [0]:
+            l1(stage, dy).start()
 
     def l2(stage, dy):
         _, _, s2, r2 = buffers(stage)
@@ -270,14 +275,15 @@
 
     def level2(stage):
         send, r1, s2, _ = buffers(stage)
-        l1(stage).wait_recv()
         for dy in range(1, chips):
             y = peer(dy)
+            l1(stage, dy).wait_recv()
             s2[dy - 1] = (send[core, y].astype(F32) + r1[y].astype(F32)).astype(BF16)
             l2(stage, dy).start()
 
     def summed(stage):
         send, r1, _, r2 = buffers(stage)
+        l1(stage, 0).wait_recv()
         total = send[core, chip].astype(F32) + r1[chip].astype(F32)
         for dy in range(1, chips):
             l2(stage, dy).wait_recv()
@@ -296,13 +302,18 @@
     def project(h, ch):
         if h == 0 and ch == 0:
             loads["wko"].wait()
-        for t in range(tp_n):
-            cols = slice(head_start(t, h), head_start(t, h) + step)
-            k_send[h * nch + ch, t % 2, t // 2] = (
-                jnp.dot(encoded[rows(ch), :], wko[:, cols], preferred_element_type=F32)
-                + kvt[rows(ch), cols]
-            ).astype(BF16)
-        l1((1, h * nch + ch)).start()
+        at = h * nch + ch
+        for dy in list(range(1, chips)) + [0]:
+            y = peer(dy)
+            for side in (other, core):
+                start = (lax.div((y * 2 + side) * KVH, tp_n) + h) * step
+                cols = pl.ds(pl.multiple_of(start, step), step)
+                k_send[at, side, y] = (
+                    jnp.dot(encoded[rows(ch), :], wko[:, cols], preferred_element_type=F32)
+                    + kvt[rows(ch), cols]
+                ).astype(BF16)
+                if side is other:
+                    l1((1, at), dy).start()
 
     def finish(h, ch):
         total = summed((1, h * nch + ch))
@@ -391,7 +402,10 @@
             query = qbuf[:, head_cols(qh)].astype(F32)
             square = jnp.mean(query * query, axis=-1, keepdims=True)
             gain = qgain_ref[...].reshape(1, HD) * (LOG2E / float(HD) ** 0.5)
-            qbuf[:, head_cols(qh)] = (query * lax.rsqrt(square + epsilon) * gain).astype(BF16)
+            query = query * lax.rsqrt(square + epsilon) * gain
+            qrows[...] = query
+            qnorm[0, :, head_cols(qh)] = query[:half].astype(BF16)
+            qnorm[1, :, head_cols(qh)] = qrows[pl.ds(texts[0], half), :].astype(BF16)
             return carry
 
         lax.fori_loop(low, high, body, 0)
@@ -407,81 +421,80 @@
             vwin[i, :, :HD] = jnp.where(valid, here[:, HD:].astype(F32) * V_SCALE, 0.0).astype(BF16)
             vwin[i, :, HD:] = jnp.where(valid, V_SCALE, 0.0).astype(BF16)
 
-    def scores(query, i):
-        return lax.dot_general(
-            query, kwin[i], (((1,), (1,)), ((), ())), preferred_element_type=F32
-        )
-
     def attend(low, high):
         row = lax.broadcasted_iota(jnp.int32, (half, 1), 0)
+        both = texts[0] + texts[1]
         first = row < texts[0]
-        live = row + half < texts[0] + texts[1]
-
-        def body(qh, carry):
-            query = qbuf[:half, head_cols(qh)]
-            both = jnp.where(first, scores(query, 0), scores(query, 1))
-            weights = jnp.exp2(both).astype(BF16)
-            result = jnp.where(
-                first,
-                jnp.dot(weights, vwin[0], preferred_element_type=F32),
-                jnp.dot(weights, vwin[1], preferred_element_type=F32),
+        top, bottom = row < both, row + half < both
+
+        def request(qh, i):
+            scores = lax.dot_general(
+                qnorm[i, :, head_cols(qh)],
+                kwin[i],
+                (((1,), (1,)), ((), ())),
+                preferred_element_type=F32,
             )
-            top = row < texts[0] + texts[1]
-            obuf[:half, head_cols(qh)] = jnp.where(top, result[:, :HD] / result[:, HD:], 0.0).astype(
-                BF16
-            )
-            query = qbuf[half:, head_cols(qh)]
-            weights = jnp.exp2(scores(query, 1)).astype(BF16)
-            result = jnp.dot(weights, vwin[1], preferred_element_type=F32)
-            obuf[half:, head_cols(qh)] = jnp.where(
-                live, result[:, :HD] / result[:, HD:], 0.0
-            ).astype(BF16)
+            weights = jnp.exp2(scores).astype(BF16)
+            result = jnp.dot(weights, vwin[i], preferred_element_type=F32)
+            return result[:, :HD] / result[:, HD:]
+
+        def body(pair, carry):
+            for slot in range(2):
+                qh = pair * 2 + slot
+                orows[slot, half : 2 * half] = request(qh, 1)
+                moved = orows[slot, pl.ds(half - texts[0], text_rows)]
+                mine = request(qh, 0)
+                out_ref[:half, head_cols(qh)] = jnp.where(
+                    first, mine, jnp.where(top, moved[:half], 0.0)
+                ).astype(BF16)
+                out_ref[half:, head_cols(qh)] = jnp.where(bottom, moved[half:], 0.0).astype(BF16)
             return carry
 
         lax.fori_loop(low, high, body, 0)
-
-    def out_copy(h):
-        cols = pl.ds(h * per_kv * HD, per_kv * HD)
-        return pltpu.make_async_copy(obuf.at[:, cols], out_hbm.at[:, cols], o_sem.at[h])
 
     loads["taps"].wait()
     for pos in range(places):
         tap_rows(pos)
     loads["wkt"].wait()
-    pieces = 4
-    done = 0
-    for pos in range(places):
-        if pos % 2 == 0:
-            tap_product(done, pieces)
-            done += 1
+
+    def part(k, of):
+        return tap_blocks * k // of
+
+    tap_product(0, part(4, 8))
+    for pos in range(per):
         x_forward(pos)
-
-    up(0)
-    down(0)
-    l1((0, 0)).start()
+        tap_product(part(4 + 2 * pos // per, 8), part(4 + 2 * (pos + 1) // per, 8))
+    layer_norm(0)
+    up(0, 0, units)
+    split = units * 3 // 5 // 256 * 256
     for ch in range(1, nch):
-        up(ch)
+        x_forward(ch * per)
+        down(ch - 1)
+        for pos in range(ch * per + 1, (ch + 1) * per):
+            x_forward(pos)
+        layer_norm(ch)
+        up(ch, 0, split)
         level2((0, ch - 1))
-        down(ch)
-        l1((0, ch)).start()
-    if done < pieces:
-        tap_product(done, pieces)
-        done += 1
+        up(ch, split, units)
+    down(nch - 1)
+    tap_product(part(6, 8), part(7, 8))
     level2((0, nch - 1))
-    while done < pieces:
-        tap_product(done, pieces)
-        done += 1
+    tap_product(part(7, 8), tap_blocks)
     loads["q"].wait()
-    norm_queries(0, q_heads)
+    norm_queries(0, per_kv)
 
     stages = [(h, ch) for h in range(kv_heads) for ch in range(nch)]
-    for j, (h, ch) in enumerate(stages):
-        if h == 0:
-            encode(ch)
-        project(h, ch)
-        if j > 0:
-            level2((1, j - 1))
-    level2((1, len(stages) - 1))
+    sent = 0
+    for ch in range(nch):
+        encode(ch)
+        for h in range(kv_heads):
+            project(h, ch)
+        if ch < nch - 1:
+            level2((1, ch))
+            sent += 1
+    for j in range(sent, len(stages)):
+        level2((1, j))
+    norm_queries(per_kv, q_heads)
 
     last = grp_n - 2
 
@@ -507,15 +520,14 @@
         base = h * per_kv
         if h + 1 < kv_heads:
             parts = last + 1
-            edges = [per_kv * p // parts for p in range(parts + 1)]
+            edges = [(base + per_kv * p // parts) // 2 for p in range(parts + 1)]
             for k in range(parts):
-                attend(base + edges[k], base + edges[k + 1])
+                attend(edges[k], edges[k + 1])
                 if k < last:
                     for pos in range(places):
                         z_hop(h + 1, pos, k)
         else:
-            attend(base, base + per_kv)
-        out_copy(h).start()
+            attend(base // 2, (base + per_kv) // 2)
 
     for pos in range(places):
         for dy in range(chips):
@@ -523,7 +535,8 @@
         for dy in range(1, chips):
             x_pass(pos, dy).wait_send()
     for stage in [(0, ch) for ch in range(nch)] + [(1, j) for j in range(len(stages))]:
-        l1(stage).wait_send()
+        for dy in range(chips):
+            l1(stage, dy).wait_send()
         for dy in range(1, chips):
             l2(stage, dy).wait_send()
     for h in range(kv_heads):
@@ -534,9 +547,6 @@
                     @pl.when(z_sends(pos, way, k))
                     def _(h=h, pos=pos, way=way, k=k):
                         z_copy(h, pos, way, k).wait_send()
-
-    for h in range(kv_heads):
-        out_copy(h).wait()
 
 
 def local(
@@ -570,6 +580,7 @@
     width = 2 * HD
     stages = kv_heads * nch
     text_rows, query_width = queries.shape
+    half = text_rows // REQ_G
     window = min(MAXT, places * grp_n) * tile
     any_spec = pl.BlockSpec(memory_space=pl.ANY)
     vmem_spec = pl.BlockSpec(memory_space=pltpu.VMEM)
@@ -578,7 +589,7 @@
     return pl.pallas_call(
         functools.partial(fused_kernel, (tp_n, grp_n, nch, chan, kv_heads)),
         name="fused",
-        out_shape=jax.ShapeDtypeStruct(queries.shape, BF16),
+        out_shape=pltpu.VMEM(queries.shape, BF16),
         in_specs=[
             any_spec,
             any_spec,
@@ -597,7 +608,7 @@
             smem_spec,
             smem_spec,
         ],
-        out_specs=any_spec,
+        out_specs=vmem_spec,
         scratch_shapes=[
             pltpu.VMEM((places, depth, tile), BF16),
             pltpu.VMEM((rc, depth), BF16),
@@ -621,7 +632,9 @@
             pltpu.VMEM((REQ_G, window, HD), BF16),
             pltpu.VMEM((REQ_G, window, 2 * HD), BF16),
             pltpu.VMEM((text_rows, query_width), BF16),
-            pltpu.VMEM((text_rows, query_width), BF16),
+            pltpu.VMEM((REQ_G, half, query_width), BF16),
+            pltpu.VMEM((text_rows, HD), F32),
+            pltpu.VMEM((2, half + text_rows, HD), F32),
         ]
         + [pltpu.VMEM((places * grp_n, tile, width), BF16) for _ in range(kv_heads)]
         + [
@@ -630,13 +643,12 @@
             dma((places, chips)),
             dma((places, chips)),
             dma((places, chips)),
-            dma((nch + stages,)),
-            dma((nch + stages,)),
+            dma((nch + stages, chips)),
+            dma((nch + stages, chips)),
             dma((nch + stages, chips - 1)),
             dma((nch + stages, chips - 1)),
             dma((kv_heads, 2, places, grp_n - 1)),
             dma((kv_heads, 2, places, grp_n - 1)),
-            dma((kv_heads,)),
         ],
         compiler_params=pltpu.CompilerParams(
             collective_id=0, has_side_effects=True, vmem_limit_bytes=VMEM_BYTES

time: 67.6 us -> 60.2 us (0.89)
  Pallas kernels: 64.2 us -> 58.7 us
  local copies, waits for them, and re-layouts: 3.16 us -> 1.32 us
    pallas_call x1, Pallas kernels: 64.2 us -> 58.7 us  [local(): pl.pallas_call(functools.partial(fused_kernel, (tp_n, grp_n, nch, chan, k...]
    unnamed x1, local copies, waits for them, and re-layouts: 3.16 us -> 1.32 us
where the time goes in v1:
time: 60.2 us; the launch traced here: 60 us
  Pallas kernels  58.7 us (98%)
  local copies, waits for them, and re-layouts  1.32 us (2%)
    pallas_call x1, Pallas kernels, local(): pl.pallas_call(functools.partial(fused_kernel, (tp_n, grp_n, nch, chan, k...  58.7 us
    unnamed x1, local copies, waits for them, and re-layouts  1.32 us

profile of v1, /device:TPU:0, one launch (start us, length us, event | category | flops | bytes accessed | tf_op | source)
XLA Modules:
  0.0 60.0 jit_solution(612224806124559776)
XLA Ops:
  0.0 58.7 %fused.1 = bf16[512,2048]{1,0:T(8,128)(2,1)S(1)} custom-call(bf16[4,320,128]{2,1,0:T(8,128)(2,1)} %bitcast.11, bf16[4,1600,128]{2,1,0:T(8,128)(2,1)} %bitcast.10, f32[1280]{0:T(1024)} %gain_ref.1, f32[1280]{0:T(1024)} %bias_ref.1, bf16[1280,1280]{1,0:T(8,128)(2,1)} %wup_hbm.1, f32[1280]{0:T(1024)} %bup_ref.1, bf16[1280,1280]{1,0:T(8,128)(2,1)} %wdn_hbm.1, ...), custom_call_target="tpu_custom_call" | custom-call | tf_op jit(solution)/shard_map/fused/pallas_call | solution.py:589
  58.7 1.3 %copy.20 = bf16[512,2048]{1,0:T(8,128)(2,1)} copy(bf16[512,2048]{1,0:T(8,128)(2,1)S(1)} %fused.1) | data formatting | bytes 4194304

commit v2 on v1

--- a/solution.py
+++ b/solution.py
@@ -66,6 +66,7 @@
     qnorm,
     qrows,
     orows,
+    obuf,
     *rest,
 ):
     tp_n, grp_n, nch, chan, kv_heads = sizes
@@ -82,6 +83,7 @@
         l2_rsem,
         z_ssem,
         z_rsem,
+        o_sem,
     ) = sems
     places, depth, tile = xg.shape
     total_tiles = places * grp_n
@@ -195,46 +197,44 @@
 
     units = hidden.shape[1]
 
-    def layer_norm(ch):
-        for pos in range(ch * per, (ch + 1) * per):
-            own_x[pos].wait()
-            x_copy(pos, 0).wait_recv()
-            for dy in range(1, chips):
-                x_pass(pos, dy).wait_recv()
-            blocks = [slice(b * HD, (b + 1) * HD) for b in range(depth // HD)]
-            total = jnp.zeros((8, tile), F32)
-            for b in blocks:
-                values = xg[pos, b, :].astype(F32)
-                total = total + jnp.sum(values.reshape(HD // 8, 8, tile), axis=0)
-            average = jnp.sum(total, axis=0, keepdims=True) / depth
-            square = jnp.zeros((8, tile), F32)
-            for b in blocks:
-                centered = xg[pos, b, :].astype(F32) - average
-                square = square + jnp.sum((centered * centered).reshape(HD // 8, 8, tile), axis=0)
-            factor = lax.rsqrt(jnp.sum(square, axis=0, keepdims=True) / depth + epsilon)
-            inside = slice((pos - ch * per) * tile, (pos - ch * per + 1) * tile)
-            for b in blocks:
-                scaled = ((xg[pos, b, :].astype(F32) - average) * factor).T
-                normed[inside, b] = (
-                    scaled * gain_ref[b].reshape(1, HD) + bias_ref[b].reshape(1, HD)
-                ).astype(BF16)
-
-    def up(ch, low, high):
-        if ch == 0 and low == 0:
+    def layer_norm(pos):
+        own_x[pos].wait()
+        x_copy(pos, 0).wait_recv()
+        for dy in range(1, chips):
+            x_pass(pos, dy).wait_recv()
+        blocks = [slice(b * HD, (b + 1) * HD) for b in range(depth // HD)]
+        total = jnp.zeros((8, tile), F32)
+        for b in blocks:
+            values = xg[pos, b, :].astype(F32)
+            total = total + jnp.sum(values.reshape(HD // 8, 8, tile), axis=0)
+        average = jnp.sum(total, axis=0, keepdims=True) / depth
+        square = jnp.zeros((8, tile), F32)
+        for b in blocks:
+            centered = xg[pos, b, :].astype(F32) - average
+            square = square + jnp.sum((centered * centered).reshape(HD // 8, 8, tile), axis=0)
+        factor = lax.rsqrt(jnp.sum(square, axis=0, keepdims=True) / depth + epsilon)
+        for b in blocks:
+            scaled = ((xg[pos, b, :].astype(F32) - average) * factor).T
+            normed[:, b] = (scaled * gain_ref[b].reshape(1, HD) + bias_ref[b].reshape(1, HD)).astype(
+                BF16
+            )
+
+    def up(pos):
+        if pos == 0:
             loads["wup"].wait()
-        for j in range(low, high, 256):
-            cols = slice(j, min(j + 256, high))
+        for j in range(0, units, 256):
+            cols = slice(j, min(j + 256, units))
             pre = jnp.dot(normed[...], wup[:, cols], preferred_element_type=F32)
             pre = pre + bup_ref[cols].reshape(1, -1)
             hidden[:, cols] = (0.5 * pre * (1.0 + lax.erf(pre * (0.5**0.5)))).astype(BF16)
 
-    def down(ch):
-        if ch == 0:
+    def down(pos):
+        if pos == 0:
             loads["wdn"].wait()
         terms = jnp.dot(hidden[...], wdn[...], preferred_element_type=F32).astype(BF16).T
         for t in range(tp_n):
-            m_send[ch, t % 2, t // 2] = terms[t * chan : (t + 1) * chan, :]
-        start_l1((0, ch))
+            m_send[pos, t % 2, t // 2] = terms[t * chan : (t + 1) * chan, :]
+        start_l1((0, pos))
 
     def buffers(stage):
         which, at = stage
@@ -244,7 +244,7 @@
 
     def number(stage):
         which, at = stage
-        return at if which == 0 else nch + at
+        return at if which == 0 else places + at
 
     def l1(stage, dy):
         send, r1, _, _ = buffers(stage)
@@ -290,14 +290,11 @@
             total = total + r2[dy - 1].astype(F32)
         return total
 
-    def encode(ch):
-        total = summed((0, ch))
-        for p in range(per):
-            pos = ch * per + p
-            here = total[:, p * tile : (p + 1) * tile] + xg[pos, share(tp_i), :].astype(F32)
-            encoded[pos * tile : (pos + 1) * tile, :] = (
-                here.T + bdn_ref[...].reshape(1, chan)
-            ).astype(BF16)
+    def encode(pos):
+        here = summed((0, pos)) + xg[pos, share(tp_i), :].astype(F32)
+        encoded[pos * tile : (pos + 1) * tile, :] = (
+            here.T + bdn_ref[...].reshape(1, chan)
+        ).astype(BF16)
 
     def project(h, ch):
         if h == 0 and ch == 0:
@@ -421,6 +418,10 @@
             vwin[i, :, :HD] = jnp.where(valid, here[:, HD:].astype(F32) * V_SCALE, 0.0).astype(BF16)
             vwin[i, :, HD:] = jnp.where(valid, V_SCALE, 0.0).astype(BF16)
 
+    def out_copy(pair):
+        cols = pl.ds(pl.multiple_of(pair * 2 * HD, HD), 2 * HD)
+        return pltpu.make_async_copy(obuf.at[pair], out_ref.at[:, cols], o_sem.at[pair])
+
     def attend(low, high):
         row = lax.broadcasted_iota(jnp.int32, (half, 1), 0)
         both = texts[0] + texts[1]
@@ -444,10 +445,12 @@
                 orows[slot, half : 2 * half] = request(qh, 1)
                 moved = orows[slot, pl.ds(half - texts[0], text_rows)]
                 mine = request(qh, 0)
-                out_ref[:half, head_cols(qh)] = jnp.where(
+                inside = slice(slot * HD, (slot + 1) * HD)
+                obuf[pair, :half, inside] = jnp.where(
                     first, mine, jnp.where(top, moved[:half], 0.0)
                 ).astype(BF16)
-                out_ref[half:, head_cols(qh)] = jnp.where(bottom, moved[half:], 0.0).astype(BF16)
+                obuf[pair, half:, inside] = jnp.where(bottom, moved[half:], 0.0).astype(BF16)
+            out_copy(pair).start()
             return carry
 
         lax.fori_loop(low, high, body, 0)
@@ -457,44 +460,46 @@
         tap_rows(pos)
     loads["wkt"].wait()
 
-    def part(k, of):
-        return tap_blocks * k // of
-
-    tap_product(0, part(4, 8))
-    for pos in range(per):
-        x_forward(pos)
-        tap_product(part(4 + 2 * pos // per, 8), part(4 + 2 * (pos + 1) // per, 8))
-    layer_norm(0)
-    up(0, 0, units)
-    split = units * 3 // 5 // 256 * 256
-    for ch in range(1, nch):
-        x_forward(ch * per)
-        down(ch - 1)
-        for pos in range(ch * per + 1, (ch + 1) * per):
-            x_forward(pos)
-        layer_norm(ch)
-        up(ch, 0, split)
-        level2((0, ch - 1))
-        up(ch, split, units)
-    down(nch - 1)
-    tap_product(part(6, 8), part(7, 8))
-    level2((0, nch - 1))
-    tap_product(part(7, 8), tap_blocks)
-    loads["q"].wait()
-    norm_queries(0, per_kv)
+    ready = tap_blocks // kv_heads
+    tap_product(0, tap_blocks // 2)
+    x_forward(0)
+    for pos in range(places):
+        layer_norm(pos)
+        up(pos)
+        if pos > 0:
+            level2((0, pos - 1))
+        if pos + 1 < places:
+            x_forward(pos + 1)
+        down(pos)
+    tapped = tap_blocks // 2 + 1
+    tap_product(tap_blocks // 2, tapped)
+    level2((0, places - 1))
+    if tapped < ready:
+        tap_product(tapped, ready)
+        tapped = ready
 
     stages = [(h, ch) for h in range(kv_heads) for ch in range(nch)]
     sent = 0
     for ch in range(nch):
-        encode(ch)
-        for h in range(kv_heads):
-            project(h, ch)
+        for pos in range(ch * per, (ch + 1) * per):
+            encode(pos)
+        project(0, ch)
         if ch < nch - 1:
             level2((1, ch))
             sent += 1
+        if ch == 0 and tapped < tap_blocks:
+            tap_product(tapped, tap_blocks)
+        if ch == nch - 1:
+            for h in range(1, kv_heads):
+                project(h, 0)
+                level2((1, sent))
+                sent += 1
+                for later in range(1, nch):
+                    project(h, later)
     for j in range(sent, len(stages)):
         level2((1, j))
-    norm_queries(per_kv, q_heads)
+    loads["q"].wait()
+    norm_queries(0, per_kv)
 
     last = grp_n - 2
 
@@ -505,6 +510,8 @@
         if h == 0:
             for ch in range(nch):
                 finish(0, ch)
+                if ch == 0:
+                    norm_queries(per_kv, q_heads)
             for k in range(last):
                 for pos in range(places):
                     z_hop(0, pos, k)
@@ -534,7 +541,7 @@
             x_copy(pos, dy).wait_send()
         for dy in range(1, chips):
             x_pass(pos, dy).wait_send()
-    for stage in [(0, ch) for ch in range(nch)] + [(1, j) for j in range(len(stages))]:
+    for stage in [(0, pos) for pos in range(places)] + [(1, j) for j in range(len(stages))]:
         for dy in range(chips):
             l1(stage, dy).wait_send()
         for dy in range(1, chips):
@@ -547,6 +554,8 @@
                     @pl.when(z_sends(pos, way, k))
                     def _(h=h, pos=pos, way=way, k=k):
                         z_copy(h, pos, way, k).wait_send()
+    for pair in range(q_heads // 2):
+        out_copy(pair).wait()
 
 
 def local(
@@ -608,11 +617,11 @@
             smem_spec,
             smem_spec,
         ],
-        out_specs=vmem_spec,
+        out_specs=any_spec,
         scratch_shapes=[
             pltpu.VMEM((places, depth, tile), BF16),
-            pltpu.VMEM((rc, depth), BF16),
-            pltpu.VMEM((rc, units), BF16),
+            pltpu.VMEM((tile, depth), BF16),
+            pltpu.VMEM((tile, units), BF16),
             pltpu.VMEM((places, tap_share, tile), BF16),
             pltpu.VMEM((n, tap_share), BF16),
             pltpu.VMEM(w_up.shape, BF16),
@@ -621,10 +630,10 @@
             pltpu.VMEM(kv_w_taps.shape, BF16),
             pltpu.VMEM((n, kv_cols), F32),
             pltpu.VMEM((n, chan), BF16),
-            pltpu.VMEM((nch, 2, chips, chan, rc), BF16),
-            pltpu.VMEM((nch, chips, chan, rc), BF16),
-            pltpu.VMEM((nch, chips - 1, chan, rc), BF16),
-            pltpu.VMEM((nch, chips - 1, chan, rc), BF16),
+            pltpu.VMEM((places, 2, chips, chan, tile), BF16),
+            pltpu.VMEM((places, chips, chan, tile), BF16),
+            pltpu.VMEM((places, chips - 1, chan, tile), BF16),
+            pltpu.VMEM((places, chips - 1, chan, tile), BF16),
             pltpu.VMEM((stages, 2, chips, rc, width), BF16),
             pltpu.VMEM((stages, chips, rc, width), BF16),
             pltpu.VMEM((stages, chips - 1, rc, width), BF16),
@@ -635,6 +644,7 @@
             pltpu.VMEM((REQ_G, half, query_width), BF16),
             pltpu.VMEM((text_rows, HD), F32),
             pltpu.VMEM((2, half + text_rows, HD), F32),
+            pltpu.VMEM((query_width // (2 * HD), text_rows, 2 * HD), BF16),
         ]
         + [pltpu.VMEM((places * grp_n, tile, width), BF16) for _ in range(kv_heads)]
         + [
@@ -643,12 +653,13 @@
             dma((places, chips)),
             dma((places, chips)),
             dma((places, chips)),
-            dma((nch + stages, chips)),
-            dma((nch + stages, chips)),
-            dma((nch + stages, chips - 1)),
-            dma((nch + stages, chips - 1)),
+            dma((places + stages, chips)),
+            dma((places + stages, chips)),
+            dma((places + stages, chips - 1)),
+            dma((places + stages, chips - 1)),
             dma((kv_heads, 2, places, grp_n - 1)),
             dma((kv_heads, 2, places, grp_n - 1)),
+            dma((query_width // (2 * HD),)),
         ],
         compiler_params=pltpu.CompilerParams(
             collective_id=0, has_side_effects=True, vmem_limit_bytes=VMEM_BYTES

time: 60.2 us -> 57.6 us (0.957)
  Pallas kernels: 58.7 us -> 56.2 us
    pallas_call x1, Pallas kernels: 58.7 us -> 56.2 us  [local(): pl.pallas_call(functools.partial(fused_kernel, (tp_n, grp_n, nch, chan, k...]
where the time goes in v2:
time: 57.6 us; the launch traced here: 57.5 us
  Pallas kernels  56.2 us (98%)
  local copies, waits for them, and re-layouts  1.32 us (2%)
    pallas_call x1, Pallas kernels, local(): pl.pallas_call(functools.partial(fused_kernel, (tp_n, grp_n, nch, chan, k...  56.2 us
    unnamed x1, local copies, waits for them, and re-layouts  1.32 us

profile of v2, /device:TPU:0, one launch (start us, length us, event | category | flops | bytes accessed | tf_op | source)
XLA Modules:
  0.0 57.5 jit_solution(12562161986093319703)
XLA Ops:
  0.0 56.2 %fused.1 = bf16[512,2048]{1,0:T(8,128)(2,1)S(1)} custom-call(bf16[4,320,128]{2,1,0:T(8,128)(2,1)} %bitcast.11, bf16[4,1600,128]{2,1,0:T(8,128)(2,1)} %bitcast.10, f32[1280]{0:T(1024)} %gain_ref.1, f32[1280]{0:T(1024)} %bias_ref.1, bf16[1280,1280]{1,0:T(8,128)(2,1)} %wup_hbm.1, f32[1280]{0:T(1024)} %bup_ref.1, bf16[1280,1280]{1,0:T(8,128)(2,1)} %wdn_hbm.1, ...), custom_call_target="tpu_custom_call" | custom-call | tf_op jit(solution)/shard_map/fused/pallas_call | solution.py:598
  56.2 1.3 %copy.20 = bf16[512,2048]{1,0:T(8,128)(2,1)} copy(bf16[512,2048]{1,0:T(8,128)(2,1)S(1)} %fused.1) | data formatting | bytes 4194304

commit v3 on v2

--- a/solution.py
+++ b/solution.py
@@ -26,16 +26,16 @@
     sizes,
     x_hbm,
     taps_hbm,
-    gain_ref,
-    bias_ref,
+    gain_hbm,
+    bias_hbm,
     wup_hbm,
-    bup_ref,
+    bup_hbm,
     wdn_hbm,
-    bdn_ref,
+    bdn_hbm,
     wko_hbm,
     wkt_hbm,
-    kgain_ref,
-    qgain_ref,
+    kgain_hbm,
+    qgain_hbm,
     q_hbm,
     tiles_ref,
     owner_ref,
@@ -67,6 +67,12 @@
     qrows,
     orows,
     obuf,
+    gain_ref,
+    bias_ref,
+    bup_ref,
+    bdn_ref,
+    kgain_ref,
+    qgain_ref,
     *rest,
 ):
     tp_n, grp_n, nch, chan, kv_heads = sizes
@@ -84,6 +90,7 @@
         z_ssem,
         z_rsem,
         o_sem,
+        s_sem,
     ) = sems
     places, depth, tile = xg.shape
     total_tiles = places * grp_n
@@ -124,10 +131,19 @@
         pltpu.make_async_copy(x_hbm.at[order[pos]], xg.at[pos, share(tp_i)], w_sem.at[6 + pos])
         for pos in range(places)
     ]
-    for c in own_x:
-        c.start()
-    for name in names:
-        loads[name].start()
+    small = [
+        pltpu.make_async_copy(src, dst, s_sem.at[i])
+        for i, (src, dst) in enumerate(
+            [
+                (gain_hbm, gain_ref),
+                (bias_hbm, bias_ref),
+                (bup_hbm, bup_ref),
+                (bdn_hbm, bdn_ref),
+                (kgain_hbm, kgain_ref),
+                (qgain_hbm, qgain_ref),
+            ]
+        )
+    ]
 
     barrier = pltpu.get_barrier_semaphore()
     pl.semaphore_signal(barrier, inc=1, device_id=partner, device_id_type=MESH)
@@ -142,6 +158,10 @@
     def _():
         pl.semaphore_signal(barrier, inc=1, device_id={"grp": grp_i + 1}, device_id_type=MESH)
 
+    for c in own_x + small:
+        c.start()
+    for name in names:
+        loads[name].start()
     neighbours = jnp.where(grp_i > 0, 1, 0) + jnp.where(grp_i < grp_n - 1, 1, 0)
     pl.semaphore_wait(barrier, chips + neighbours)
 
@@ -323,7 +343,9 @@
             at = order[pos] * grp_n + grp_i
             kvs[h][at, :, :HD] = key[p * tile : (p + 1) * tile]
             kvs[h][at, :, HD:] = value[p * tile : (p + 1) * tile]
-            z_start(h, pos, 0)
+        for pos, way in travels(h):
+            if pos // per == ch:
+                z_start(h, pos, way, 0)
 
     def reaches_up(index, q):
         return (index >= REQ_G * q) & (index >= total_tiles - CAP * (grp_n - q))
@@ -355,22 +377,33 @@
             return (grp_i - k - 1 >= 0) & reaches_up(base + grp_i - k - 1, grp_i)
         return (grp_i + k + 1 <= grp_n - 1) & reaches_down(base + grp_i + k + 1, grp_i)
 
-    def z_start(h, pos, k):
-        for way in range(2):
-
-            @pl.when(z_sends(pos, way, k))
-            def _(way=way):
-                z_copy(h, pos, way, k).start()
-
-    def z_hop(h, pos, k):
-        for way in range(2):
+    def z_start(h, pos, way, k):
+        @pl.when(z_sends(pos, way, k))
+        def _():
+            z_copy(h, pos, way, k).start()
+
+    def chunks(h):
+        return range(nch) if h == 0 else range(nch - 1, -1, -1)
+
+    def travels(h):
+        found = []
+        for ch in chunks(h):
+            here = list(range(ch * per, (ch + 1) * per))
+            up_way = sorted(here, key=lambda pos: -order[pos])
+            down_way = sorted(here, key=lambda pos: order[pos])
+            for p in range(per):
+                found += [(up_way[p], 0), (down_way[p], 1)]
+        return found
+
+    def z_hop(h, k):
+        for pos, way in travels(h):
 
             @pl.when(z_gets(pos, way, k))
-            def _(way=way):
+            def _(pos=pos, way=way):
                 z_copy(h, pos, way, k).wait_recv()
 
-        if k + 1 < grp_n - 1:
-            z_start(h, pos, k + 1)
+            if k + 1 < grp_n - 1:
+                z_start(h, pos, way, k + 1)
 
     text_rows = qbuf.shape[0]
     q_heads = qbuf.shape[1] // HD
@@ -455,6 +488,8 @@
 
         lax.fori_loop(low, high, body, 0)
 
+    for c in small:
+        c.wait()
     loads["taps"].wait()
     for pos in range(places):
         tap_rows(pos)
@@ -478,51 +513,53 @@
         tap_product(tapped, ready)
         tapped = ready
 
-    stages = [(h, ch) for h in range(kv_heads) for ch in range(nch)]
-    sent = 0
-    for ch in range(nch):
+    def more_taps(count):
+        nonlocal tapped
+        count = min(count, tap_blocks - tapped)
+        if count > 0:
+            tap_product(tapped, tapped + count)
+            tapped += count
+
+    def encode_chunk(ch):
         for pos in range(ch * per, (ch + 1) * per):
             encode(pos)
+
+    stages = [(h, ch) for h in range(kv_heads) for ch in range(nch)]
+    encode_chunk(0)
+    project(0, 0)
+    more_taps(1)
+    level2((1, 0))
+    for ch in range(1, nch):
+        encode_chunk(ch)
         project(0, ch)
-        if ch < nch - 1:
-            level2((1, ch))
-            sent += 1
-        if ch == 0 and tapped < tap_blocks:
-            tap_product(tapped, tap_blocks)
-        if ch == nch - 1:
-            for h in range(1, kv_heads):
-                project(h, 0)
-                level2((1, sent))
-                sent += 1
-                for later in range(1, nch):
-                    project(h, later)
-    for j in range(sent, len(stages)):
-        level2((1, j))
+        more_taps(1)
+        level2((1, ch))
+    more_taps(tap_blocks)
+    pending = [(h, ch) for h in range(1, kv_heads) for ch in chunks(h)]
+    if pending:
+        project(*pending[0])
+    finish(0, 0)
+    for j, (h, ch) in enumerate(pending):
+        if j + 1 < len(pending):
+            project(*pending[j + 1])
+        level2((1, h * nch + ch))
     loads["q"].wait()
     norm_queries(0, per_kv)
-
+    for ch in range(1, nch):
+        finish(0, ch)
     last = grp_n - 2
-
-    def chunk(ch):
-        return range(ch * per, (ch + 1) * per)
-
     for h in range(kv_heads):
         if h == 0:
-            for ch in range(nch):
-                finish(0, ch)
-                if ch == 0:
+            coming = pending[:nch]
+            for k in range(last):
+                z_hop(0, k)
+                if k == 0:
                     norm_queries(per_kv, q_heads)
-            for k in range(last):
-                for pos in range(places):
-                    z_hop(0, pos, k)
-                for ch in range(nch):
-                    if kv_heads > 1 and k == ch:
-                        finish(1, ch)
-        if h == 0 and kv_heads > 1:
-            for ch in range(last, nch):
-                finish(1, ch)
-        for pos in range(places):
-            z_hop(h, pos, last)
+                if coming:
+                    finish(*coming.pop(0))
+            while coming:
+                finish(*coming.pop(0))
+        z_hop(h, last)
         windows(h)
         base = h * per_kv
         if h + 1 < kv_heads:
@@ -531,8 +568,7 @@
             for k in range(parts):
                 attend(edges[k], edges[k + 1])
                 if k < last:
-                    for pos in range(places):
-                        z_hop(h + 1, pos, k)
+                    z_hop(h + 1, k)
         else:
             attend(base // 2, (base + per_kv) // 2)
 
@@ -592,7 +628,6 @@
     half = text_rows // REQ_G
     window = min(MAXT, places * grp_n) * tile
     any_spec = pl.BlockSpec(memory_space=pl.ANY)
-    vmem_spec = pl.BlockSpec(memory_space=pltpu.VMEM)
     smem_spec = pl.BlockSpec(memory_space=pltpu.SMEM)
     dma = pltpu.SemaphoreType.DMA
     return pl.pallas_call(
@@ -600,19 +635,7 @@
         name="fused",
         out_shape=pltpu.VMEM(queries.shape, BF16),
         in_specs=[
-            any_spec,
-            any_spec,
-            vmem_spec,
-            vmem_spec,
-            any_spec,
-            vmem_spec,
-            any_spec,
-            vmem_spec,
-            any_spec,
-            any_spec,
-            vmem_spec,
-            vmem_spec,
-            any_spec,
+            *[any_spec] * 13,
             smem_spec,
             smem_spec,
             smem_spec,
@@ -646,6 +669,7 @@
             pltpu.VMEM((2, half + text_rows, HD), F32),
             pltpu.VMEM((query_width // (2 * HD), text_rows, 2 * HD), BF16),
         ]
+        + [pltpu.VMEM(a.shape, F32) for a in (ln_gain, ln_bias, b_up, b_down, k_gain, q_gain)]
         + [pltpu.VMEM((places * grp_n, tile, width), BF16) for _ in range(kv_heads)]
         + [
             dma((6 + places,)),
@@ -660,6 +684,7 @@
             dma((kv_heads, 2, places, grp_n - 1)),
             dma((kv_heads, 2, places, grp_n - 1)),
             dma((query_width // (2 * HD),)),
+            dma((6,)),
         ],
         compiler_params=pltpu.CompilerParams(
             collective_id=0, has_side_effects=True, vmem_limit_bytes=VMEM_BYTES

time: 57.6 us -> 59.1 us (1.026)
  Pallas kernels: 56.2 us -> 57.6 us
    pallas_call x1, Pallas kernels: 56.2 us -> 57.6 us  [local(): pl.pallas_call(functools.partial(fused_kernel, (tp_n, grp_n, nch, chan, k...]
where the time goes in v3:
time: 59.1 us; the launch traced here: 58.9 us
  Pallas kernels  57.6 us (97%)
  local copies, waits for them, and re-layouts  1.32 us (2%)
    pallas_call x1, Pallas kernels, local(): pl.pallas_call(functools.partial(fused_kernel, (tp_n, grp_n, nch, chan, k...  57.6 us
    unnamed x1, local copies, waits for them, and re-layouts  1.32 us

profile of v3, /device:TPU:0, one launch (start us, length us, event | category | flops | bytes accessed | tf_op | source)
XLA Modules:
  0.0 58.9 jit_solution(7649442482439516906)
XLA Ops:
  0.0 57.6 %fused.1 = bf16[512,2048]{1,0:T(8,128)(2,1)S(1)} custom-call(bf16[4,320,128]{2,1,0:T(8,128)(2,1)} %bitcast.11, bf16[4,1600,128]{2,1,0:T(8,128)(2,1)} %bitcast.10, f32[1280]{0:T(1024)} %gain_hbm.1, f32[1280]{0:T(1024)} %bias_hbm.1, bf16[1280,1280]{1,0:T(8,128)(2,1)} %wup_hbm.1, f32[1280]{0:T(1024)} %bup_hbm.1, bf16[1280,1280]{1,0:T(8,128)(2,1)} %wdn_hbm.1, ...), custom_call_target="tpu_custom_call" | custom-call | tf_op jit(solution)/shard_map/fused/pallas_call | solution.py:633
  57.6 1.3 %copy.20 = bf16[512,2048]{1,0:T(8,128)(2,1)} copy(bf16[512,2048]{1,0:T(8,128)(2,1)S(1)} %fused.1) | data formatting | bytes 4194304

commit v4 on v3

--- a/solution.py
+++ b/solution.py
@@ -26,16 +26,16 @@
     sizes,
     x_hbm,
     taps_hbm,
-    gain_hbm,
-    bias_hbm,
+    gain_ref,
+    bias_ref,
     wup_hbm,
-    bup_hbm,
+    bup_ref,
     wdn_hbm,
-    bdn_hbm,
+    bdn_ref,
     wko_hbm,
     wkt_hbm,
-    kgain_hbm,
-    qgain_hbm,
+    kgain_ref,
+    qgain_ref,
     q_hbm,
     tiles_ref,
     owner_ref,
@@ -67,12 +67,6 @@
     qrows,
     orows,
     obuf,
-    gain_ref,
-    bias_ref,
-    bup_ref,
-    bdn_ref,
-    kgain_ref,
-    qgain_ref,
     *rest,
 ):
     tp_n, grp_n, nch, chan, kv_heads = sizes
@@ -90,7 +84,6 @@
         z_ssem,
         z_rsem,
         o_sem,
-        s_sem,
     ) = sems
     places, depth, tile = xg.shape
     total_tiles = places * grp_n
@@ -131,19 +124,10 @@
         pltpu.make_async_copy(x_hbm.at[order[pos]], xg.at[pos, share(tp_i)], w_sem.at[6 + pos])
         for pos in range(places)
     ]
-    small = [
-        pltpu.make_async_copy(src, dst, s_sem.at[i])
-        for i, (src, dst) in enumerate(
-            [
-                (gain_hbm, gain_ref),
-                (bias_hbm, bias_ref),
-                (bup_hbm, bup_ref),
-                (bdn_hbm, bdn_ref),
-                (kgain_hbm, kgain_ref),
-                (qgain_hbm, qgain_ref),
-            ]
-        )
-    ]
+    for c in own_x:
+        c.start()
+    for name in names:
+        loads[name].start()
 
     barrier = pltpu.get_barrier_semaphore()
     pl.semaphore_signal(barrier, inc=1, device_id=partner, device_id_type=MESH)
@@ -158,10 +142,6 @@
     def _():
         pl.semaphore_signal(barrier, inc=1, device_id={"grp": grp_i + 1}, device_id_type=MESH)
 
-    for c in own_x + small:
-        c.start()
-    for name in names:
-        loads[name].start()
     neighbours = jnp.where(grp_i > 0, 1, 0) + jnp.where(grp_i < grp_n - 1, 1, 0)
     pl.semaphore_wait(barrier, chips + neighbours)
 
@@ -320,17 +300,14 @@
         if h == 0 and ch == 0:
             loads["wko"].wait()
         at = h * nch + ch
-        for dy in list(range(1, chips)) + [0]:
-            y = peer(dy)
-            for side in (other, core):
-                start = (lax.div((y * 2 + side) * KVH, tp_n) + h) * step
-                cols = pl.ds(pl.multiple_of(start, step), step)
-                k_send[at, side, y] = (
-                    jnp.dot(encoded[rows(ch), :], wko[:, cols], preferred_element_type=F32)
-                    + kvt[rows(ch), cols]
-                ).astype(BF16)
-                if side is other:
-                    l1((1, at), dy).start()
+        for t in range(tp_n):
+            start = (t * KVH // tp_n + h) * step
+            cols = slice(start, start + step)
+            k_send[at, t % 2, t // 2] = (
+                jnp.dot(encoded[rows(ch), :], wko[:, cols], preferred_element_type=F32)
+                + kvt[rows(ch), cols]
+            ).astype(BF16)
+        start_l1((1, at))
 
     def finish(h, ch):
         total = summed((1, h * nch + ch))
@@ -395,8 +372,8 @@
                 found += [(up_way[p], 0), (down_way[p], 1)]
         return found
 
-    def z_hop(h, k):
-        for pos, way in travels(h):
+    def z_hop(h, k, low=0, high=None):
+        for pos, way in travels(h)[low:high]:
 
             @pl.when(z_gets(pos, way, k))
             def _(pos=pos, way=way):
@@ -488,15 +465,14 @@
 
         lax.fori_loop(low, high, body, 0)
 
-    for c in small:
-        c.wait()
     loads["taps"].wait()
     for pos in range(places):
         tap_rows(pos)
     loads["wkt"].wait()
 
     ready = tap_blocks // kv_heads
-    tap_product(0, tap_blocks // 2)
+    tapped = tap_blocks * 5 // 8
+    tap_product(0, tapped)
     x_forward(0)
     for pos in range(places):
         layer_norm(pos)
@@ -506,19 +482,10 @@
         if pos + 1 < places:
             x_forward(pos + 1)
         down(pos)
-    tapped = tap_blocks // 2 + 1
-    tap_product(tap_blocks // 2, tapped)
-    level2((0, places - 1))
     if tapped < ready:
         tap_product(tapped, ready)
         tapped = ready
-
-    def more_taps(count):
-        nonlocal tapped
-        count = min(count, tap_blocks - tapped)
-        if count > 0:
-            tap_product(tapped, tapped + count)
-            tapped += count
+    level2((0, places - 1))
 
     def encode_chunk(ch):
         for pos in range(ch * per, (ch + 1) * per):
@@ -527,24 +494,23 @@
     stages = [(h, ch) for h in range(kv_heads) for ch in range(nch)]
     encode_chunk(0)
     project(0, 0)
-    more_taps(1)
     level2((1, 0))
+    if tapped < tap_blocks:
+        tap_product(tapped, tap_blocks)
+    pending = [(h, ch) for h in range(1, kv_heads) for ch in chunks(h)]
     for ch in range(1, nch):
         encode_chunk(ch)
         project(0, ch)
-        more_taps(1)
+    for later in pending:
+        project(*later)
+    for ch in range(1, nch):
         level2((1, ch))
-    more_taps(tap_blocks)
-    pending = [(h, ch) for h in range(1, kv_heads) for ch in chunks(h)]
-    if pending:
-        project(*pending[0])
     finish(0, 0)
-    for j, (h, ch) in enumerate(pending):
-        if j + 1 < len(pending):
-            project(*pending[j + 1])
+    for h, ch in pending:
         level2((1, h * nch + ch))
     loads["q"].wait()
-    norm_queries(0, per_kv)
+    norm_queries(0, q_heads)
+    z_hop(0, 0, 0, 2)
     for ch in range(1, nch):
         finish(0, ch)
     last = grp_n - 2
@@ -552,9 +518,7 @@
         if h == 0:
             coming = pending[:nch]
             for k in range(last):
-                z_hop(0, k)
-                if k == 0:
-                    norm_queries(per_kv, q_heads)
+                z_hop(0, k, 2 if k == 0 else 0)
                 if coming:
                     finish(*coming.pop(0))
             while coming:
@@ -628,6 +592,7 @@
     half = text_rows // REQ_G
     window = min(MAXT, places * grp_n) * tile
     any_spec = pl.BlockSpec(memory_space=pl.ANY)
+    vmem_spec = pl.BlockSpec(memory_space=pltpu.VMEM)
     smem_spec = pl.BlockSpec(memory_space=pltpu.SMEM)
     dma = pltpu.SemaphoreType.DMA
     return pl.pallas_call(
@@ -635,7 +600,19 @@
         name="fused",
         out_shape=pltpu.VMEM(queries.shape, BF16),
         in_specs=[
-            *[any_spec] * 13,
+            any_spec,
+            any_spec,
+            vmem_spec,
+            vmem_spec,
+            any_spec,
+            vmem_spec,
+            any_spec,
+            vmem_spec,
+            any_spec,
+            any_spec,
+            vmem_spec,
+            vmem_spec,
+            any_spec,
             smem_spec,
             smem_spec,
             smem_spec,
@@ -669,7 +646,6 @@
             pltpu.VMEM((2, half + text_rows, HD), F32),
             pltpu.VMEM((query_width // (2 * HD), text_rows, 2 * HD), BF16),
         ]
-        + [pltpu.VMEM(a.shape, F32) for a in (ln_gain, ln_bias, b_up, b_down, k_gain, q_gain)]
         + [pltpu.VMEM((places * grp_n, tile, width), BF16) for _ in range(kv_heads)]
         + [
             dma((6 + places,)),
@@ -684,7 +660,6 @@
             dma((kv_heads, 2, places, grp_n - 1)),
             dma((kv_heads, 2, places, grp_n - 1)),
             dma((query_width // (2 * HD),)),
-            dma((6,)),
         ],
         compiler_params=pltpu.CompilerParams(
             collective_id=0, has_side_effects=True, vmem_limit_bytes=VMEM_BYTES

time: 59.1 us -> 56.4 us (0.954)
  Pallas kernels: 57.6 us -> 54.9 us
    pallas_call x1, Pallas kernels: 57.6 us -> 54.9 us  [local(): pl.pallas_call(functools.partial(fused_kernel, (tp_n, grp_n, nch, chan, k...]
where the time goes in v4:
time: 56.4 us; the launch traced here: 56.2 us
  Pallas kernels  54.9 us (97%)
  local copies, waits for them, and re-layouts  1.32 us (2%)
    pallas_call x1, Pallas kernels, local(): pl.pallas_call(functools.partial(fused_kernel, (tp_n, grp_n, nch, chan, k...  54.9 us
    unnamed x1, local copies, waits for them, and re-layouts  1.32 us

profile of v4, /device:TPU:0, one launch (start us, length us, event | category | flops | bytes accessed | tf_op | source)
XLA Modules:
  0.0 56.2 jit_solution(7298460664163460371)
XLA Ops:
  0.0 54.9 %fused.1 = bf16[512,2048]{1,0:T(8,128)(2,1)S(1)} custom-call(bf16[4,320,128]{2,1,0:T(8,128)(2,1)} %bitcast.11, bf16[4,1600,128]{2,1,0:T(8,128)(2,1)} %bitcast.10, f32[1280]{0:T(1024)} %gain_ref.1, f32[1280]{0:T(1024)} %bias_ref.1, bf16[1280,1280]{1,0:T(8,128)(2,1)} %wup_hbm.1, f32[1280]{0:T(1024)} %bup_ref.1, bf16[1280,1280]{1,0:T(8,128)(2,1)} %wdn_hbm.1, ...), custom_call_target="tpu_custom_call" | custom-call | tf_op jit(solution)/shard_map/fused/pallas_call | solution.py:598
  54.9 1.3 %copy.20 = bf16[512,2048]{1,0:T(8,128)(2,1)} copy(bf16[512,2048]{1,0:T(8,128)(2,1)S(1)} %fused.1) | data formatting | bytes 4194304
